TPU v7x, 32 devices: a whole 2x2x4 slice. The times are simulated.
32 devices in a mesh: tm: 8 (over y, x, core), chan: 4 (over z).
Axes of the slice: x: 2, y: 2, z: 4, core: 2. Of those that a mesh axis runs over, the one named last changes fastest.
Arguments:
- volts: bfloat16 [4, 16, 12288, 256], P(None, 'chan', 'tm'), may hold values from -6 to 6
- delay_peak: int32 [128, 128], P('tm', 'chan'), may hold values from 0 to 32767
- rate_peak: int32 [128, 128], P('tm', 'chan'), may hold values from 0 to 15
- station_order: int32 [128], replicated, may hold values from 0 to 127, each once
- ref_station: int32 [1], replicated, may hold values from 0 to 63
Outputs:
- fringe: float32 [128, 128, 2, 8], P('tm', 'chan')
- normal: float32 [128, 2, 256], P('tm', None, 'chan')
- rhs: float32 [128, 2], P('tm')
Inputs may be any that keep to these rules, and one draw needn't show every extreme that they name: `station_order`: each input appears once.
All inputs are finite; a program needn't handle non-finite values.
Results may differ from a plain program's by a relative error of at most 0.0003.
Values sent between devices are 32-bit elements; how exact they have to be, the bound alone decides.
A program may use at most 64 MiB of HBM per device.

v0:
```python
import math
import jax
import jax.numpy as jnp
from jax import lax
from jax.sharding import PartitionSpec as P

BAND = 16384
PERIODS_ALL = 8
WD = 4
WR = 2


def fringe_window(vis_re, vis_im, dpeak, rpeak, chans_total, periods):
    chan_local = vis_re.shape[3]
    dgrid = 2 * BAND
    rgrid = 2 * PERIODS_ALL
    dstep = BAND // chans_total
    rstep = PERIODS_ALL // periods
    chan_idx = jnp.arange(chan_local, dtype=jnp.int32)
    period_idx = jnp.arange(periods, dtype=jnp.int32)
    delays = dpeak[:, :, None] + (jnp.arange(WD, dtype=jnp.int32) - WD // 2) * dstep
    rates = rpeak[:, :, None] + (jnp.arange(WR, dtype=jnp.int32) - WR // 2) * rstep
    dphase = jnp.mod(delays[..., None] * chan_idx, dgrid).astype(jnp.float32) * (
        2.0 * math.pi / dgrid
    )
    rphase = jnp.mod(rates[..., None] * period_idx, rgrid).astype(jnp.float32) * (
        2.0 * math.pi / rgrid
    )
    angle = rphase[:, :, :, None, :, None] + dphase[:, :, None, :, None, :]
    cosine = jnp.cos(angle)
    sine = jnp.sin(angle)
    vr = vis_re[:, :, None, None]
    vi = vis_im[:, :, None, None]
    fre = jnp.sum(vr * cosine + vi * sine, axis=(4, 5))
    fim = jnp.sum(vi * cosine - vr * sine, axis=(4, 5))
    return (fre, fim)


def baseline_weights(fre, fim):
    power = fre * fre + fim * fim
    udel = (2.0 * jnp.arange(WD, dtype=jnp.float32) + 1.0 - WD) / WD
    urat = (2.0 * jnp.arange(WR, dtype=jnp.float32) + 1.0 - WR) / WR
    udel = udel[None, :]
    urat = urat[:, None]
    m_dd = jnp.mean(power * udel * udel, axis=(2, 3))
    m_dr = jnp.mean(power * udel * urat, axis=(2, 3))
    m_rr = jnp.mean(power * urat * urat, axis=(2, 3))
    g_d = jnp.mean(power * udel, axis=(2, 3))
    g_r = jnp.mean(power * urat, axis=(2, 3))
    return jnp.stack([m_dd, m_dr, m_rr, g_d, g_r])


def normal_terms(weights, row_inputs, col_inputs, inputs):
    slots = jnp.arange(inputs, dtype=jnp.int32)
    incidence = (row_inputs[:, None, None] == slots).astype(jnp.float32) - (
        col_inputs[None, :, None] == slots
    ).astype(jnp.float32)
    flat = incidence.reshape(-1, inputs)

    def block(weight):
        scaled = (incidence * weight[:, :, None]).reshape(-1, inputs)
        return jnp.dot(scaled.T, flat, precision=lax.Precision.HIGHEST) / inputs

    n_dd = block(weights[0])
    n_dr = block(weights[1])
    n_rr = block(weights[2])
    normal = jnp.concatenate(
        [jnp.concatenate([n_dd, n_dr], 1), jnp.concatenate([n_dr, n_rr], 1)], 0
    )
    rhs_d = jnp.dot(weights[3].reshape(-1), flat, precision=lax.Precision.HIGHEST) / inputs
    rhs_r = jnp.dot(weights[4].reshape(-1), flat, precision=lax.Precision.HIGHEST) / inputs
    return (normal, jnp.concatenate([rhs_d, rhs_r]))


def full_gram(volts, inputs, scale):
    prod = jnp.einsum("acti,actj->iacj", volts, volts, preferred_element_type=jnp.float32)
    real = prod[:inputs, :, :, :inputs] + prod[inputs:, :, :, inputs:]
    imag = prod[:inputs, :, :, inputs:] - prod[inputs:, :, :, :inputs]
    return jnp.stack([real, imag], axis=3) * scale


def body(volts, delay_peak, rate_peak, station_order, ref_station):
    periods, chans, samples, width = volts.shape
    inputs = width // 2
    row_count = delay_peak.shape[0]
    col_count = delay_peak.shape[1]
    time_devs = lax.axis_size("tm")
    chan_devs = lax.axis_size("chan")
    chans_total = chans * chan_devs
    scale = float(samples * time_devs) ** (-0.5)
    spread = float(periods * chans_total) ** (-0.5)
    col_inputs = lax.dynamic_slice_in_dim(
        station_order, lax.axis_index("chan") * col_count, col_count
    )
    row_inputs = lax.axis_index("tm") * row_count + jnp.arange(row_count, dtype=jnp.int32)
    gram = full_gram(volts, inputs, scale)
    summed = lax.psum_scatter(
        gram.reshape(lax.axis_size("tm") * row_count, -1), "tm", scatter_dimension=0, tiled=True
    )
    vis = summed.reshape(row_count, periods, chans, 2, inputs)
    grouped = jnp.take(vis, station_order, axis=4)
    moved = lax.all_to_all(grouped, "chan", split_axis=4, concat_axis=2, tiled=True)
    vis_re = jnp.transpose(moved[:, :, :, 0], (0, 3, 1, 2))
    vis_im = jnp.transpose(moved[:, :, :, 1], (0, 3, 1, 2))
    fre, fim = fringe_window(vis_re, vis_im, delay_peak, rate_peak, chans_total, periods)
    auto = (row_inputs[:, None] == col_inputs[None, :])[:, :, None, None]
    fre = jnp.where(auto, 0.0, fre * spread)
    fim = jnp.where(auto, 0.0, fim * spread)
    fringe = jnp.stack([fre, fim], axis=2).reshape(row_count, col_count, 2, WR * WD)
    weights = baseline_weights(fre, fim)
    col_width = 2 * inputs // chan_devs
    normal_part, rhs_part = normal_terms(weights, row_inputs, col_inputs, inputs)
    arranged = jnp.transpose(normal_part.reshape(2, inputs, 2 * inputs), (1, 0, 2))
    arranged = arranged.reshape(time_devs, row_count, 2, chan_devs, col_width)
    arranged = jnp.transpose(arranged, (0, 3, 1, 2, 4)).reshape(
        time_devs * chan_devs * row_count, 2, col_width
    )
    normal_rows = lax.psum_scatter(arranged, ("tm", "chan"), scatter_dimension=0, tiled=True)
    rhs_all = lax.psum(jnp.transpose(rhs_part.reshape(2, inputs), (1, 0)), ("tm", "chan"))
    rhs_rows = lax.dynamic_slice_in_dim(rhs_all, lax.axis_index("tm") * row_count, row_count, 0)
    columns = lax.axis_index("chan") * col_width + jnp.arange(col_width, dtype=jnp.int32)
    params = jnp.arange(2, dtype=jnp.int32)[None, :] * inputs + row_inputs[:, None]
    row_ref = row_inputs // 2 == ref_station[0]
    col_ref = columns % inputs // 2 == ref_station[0]
    ident = (params[:, :, None] == columns[None, None, :]).astype(jnp.float32)
    normal_rows = jnp.where(row_ref[:, None, None] | col_ref[None, None, :], ident, normal_rows)
    rhs_rows = jnp.where(row_ref[:, None], 0.0, rhs_rows)
    return (fringe, normal_rows, rhs_rows)


def solution(mesh):
    in_specs = (P(None, "chan", "tm", None), P("tm", "chan"), P("tm", "chan"), P(), P())
    out_specs = (P("tm", "chan", None, None), P("tm", None, "chan"), P("tm", None))
    return jax.shard_map(body, mesh=mesh, in_specs=in_specs, out_specs=out_specs, check_vma=False)
```

profile of v0, /device:TPU:0, one launch (start us, length us, event | category | flops | bytes accessed | tf_op | source)
XLA Modules:
  0.0 298.8 jit_solution(5013165204191400454)
XLA Ops:
  7.2 11.0 %convolution_bitcast_fusion = f32[256,4,4,256]{0,3,2,1:T(8,128)S(1)} fusion(bf16[4,4,1536,256]{3,2,1,0:T(8,128)(2,1)} %param.5), kind=kOutput, calls=%fused_computation.11 | convolution fusion | flops 3221225472 | bytes 16777216 | tf_op jit(solution)/shard_map/acti,actj->iacj/dot_general | solution.py:76
  19.0 1.9 copy.56
  22.3 42.6 %reduce-scatter.7.cloned.1.call-done = f32[16,4096]{1,0:T(8,128)} async-done(((f32[128,4096]{1,0:T(8,128)}), f32[16,4096]{1,0:T(8,128)}) %reduce-scatter.7.cloned.1.call-update) | async-done | bytes 262160
  64.9 1.5 copy.57
  66.5 2.7 copy.41
  69.2 4.9 %gather_fusion = f32[128,16,4,4,2]{1,3,4,2,0:T(4,128)} fusion(f32[16,4,4,2,128]{0,2,4,3,1:T(4,128)} %copy.41, s32[1024]{0:T(1024)S(1)} %pad_clamp_fusion), kind=kCustom, calls=%fused_computation | custom fusion | bytes 524800 | tf_op jit(solution)/shard_map/jit(_take)/gather | solution.py:101
  74.1 2.1 fusion.47
  76.2 2.3 reshape.374
  78.5 4.6 %all-to-all-start = ((f32[4,1,16384]{2,1,0:T(1,128)}), f32[4,1,16384]{2,1,0:T(1,128)S(1)}, u32[]{:S(2)}, u32[]{:S(2)}) async-start(f32[4,1,16384]{2,1,0:T(1,128)} %reshape.374), calls=%async_computation | async-start | bytes 524288 | tf_op jit(solution)/shard_map/all_to_all | solution.py:102
  83.1 1.0 fusion.22
  84.2 7.9 %all-to-all-done = f32[4,1,16384]{2,1,0:T(1,128)S(1)} async-done(((f32[4,1,16384]{2,1,0:T(1,128)}), f32[4,1,16384]{2,1,0:T(1,128)S(1)}, u32[]{:S(2)}, u32[]{:S(2)}) %all-to-all-start) | async-done | bytes 262176 | tf_op jit(solution)/shard_map/all_to_all | solution.py:102
  92.5 1.4 reduce
  93.9 1.5 reshape.375
  95.4 1.0 copy.42
  97.4 16.5 %fusion.5 = (f32[16,32,2,4]{1,3,2,0:T(4,128)S(1)}, f32[16,32,2,4]{1,3,2,0:T(4,128)S(1)}) fusion(f32[16,32,4,16]{1,3,2,0:T(8,128)S(1)} %copy.44, f32[16,32,4,16]{1,3,2,0:T(8,128)S(1)} %copy-done, f32[16,32,2,4]{1,3,2,0:T(4,128)S(1)} %fusion.41, f32[16,32,4,16]{1,3,2,0:T(8,128)S(1)} %copy.43), kind=kLoop, calls=%fused_computation.8 | loop fusion | flops 2351104 | bytes 442368 | tf_op jit(solution)/shard_map/reduce_sum | solution.py:34
  114.8 37.9 %psum.7 = f32[128,2]{0,1:T(2,128)S(1)} all-reduce(f32[128,2]{0,1:T(2,128)S(1)} %maximum_bitcast_fusion), channel_id=1, replica_groups=mesh['tm'=8,'chan'=4] {'tm','chan'}, use_global_device_ids=true, to_apply=%region_9.10 | all-reduce | flops 256 | bytes 2048 | tf_op jit(solution)/shard_map/psum | solution.py:119
  152.7 0.7 fusion.9
  153.4 0.7 fusion.8
  154.1 0.7 fusion.10
  155.2 0.8 copy.48
  156.0 0.7 pad_maximum_fusion
  156.7 0.6 dynamic-slice_select_fusion
  157.3 133.2 %reduce-scatter.5.cloned.1.call-done = f32[16,2,64]{2,0,1:T(8,128)} async-done(((f32[512,2,64]{2,0,1:T(8,128)}), f32[16,2,64]{2,0,1:T(8,128)}) %reduce-scatter.5.cloned.1.call-update) | async-done | bytes 8208 | tf_op jit(solution)/shard_map/reduce_scatter | solution.py:118
  290.6 0.8 convert_select_fusion
  (53 shorter events, 5.0 us)
Async XLA Ops:
  7.2 57.8 %reduce-scatter.7.cloned.1.call-start = ((), (), s32[]{:S(2)}) async-start(), calls=%async_computation.4 | async-start | bytes 2359296
  19.0 2.6 copy-start.3
  19.0 3.1 %copy-start.1 = (s32[16,32]{1,0:T(8,128)S(1)}, s32[16,32]{1,0:T(8,128)}, u32[]{:S(2)}) copy-start(s32[16,32]{1,0:T(8,128)} %param.7) | copy-start | bytes 6148
  19.0 3.2 %copy-start.2 = (s32[16,32]{1,0:T(8,128)S(1)}, s32[16,32]{1,0:T(8,128)}, u32[]{:S(2)}) copy-start(s32[16,32]{1,0:T(8,128)} %param.6) | copy-start | bytes 6148
  78.5 13.5 %all-to-all-start = ((f32[4,1,16384]{2,1,0:T(1,128)}), f32[4,1,16384]{2,1,0:T(1,128)S(1)}, u32[]{:S(2)}, u32[]{:S(2)}) async-start(f32[4,1,16384]{2,1,0:T(1,128)} %reshape.374), calls=%async_computation | async-start | bytes 524288 | tf_op jit(solution)/shard_map/all_to_all | solution.py:102
  83.1 207.5 %reduce-scatter.5.cloned.1.call-start = ((), (), s32[]{:S(2)}) async-start(), calls=%async_computation.3 | async-start | bytes 540672 | tf_op jit(solution)/shard_map/reduce_scatter | solution.py:118
  96.4 1.0 copy-start
Sparse Core Ops, SparseCore 0:
  21.0 43.8 reduce-scatter.6
  156.1 134.3 reduce-scatter.4
where the time goes:
time: 299 us
  waiting for transfers between devices  184 us (62%)
  blocking collectives  37.9 us (13%)
  other arithmetic  24.6 us (8%)
  local copies, waits for them, and re-layouts  19.4 us (6%)
  between operations  15 us (5%)
  matrix products  13.6 us (5%)
  starting transfers between devices  4.65 us (2%)
    reduce_scatter x1, waiting for transfers between devices, body(): lax.psum_scatter(arranged, ('tm', 'chan'), scatter_dimension=0, tiled=True)  133 us
    unnamed x3, waiting for transfers between devices  42.6 us
    psum x1, blocking collectives, body(): lax.psum(jnp.transpose(rhs_part.reshape(2, inputs), (1, 0)), ('tm', 'chan'))  37.9 us
    reduce_sum x1, other arithmetic, fringe_window(): fre = jnp.sum(vr * cosine + vi * sine, axis=(4, 5))  16.5 us
    dot_general x1, matrix products, full_gram(): jnp.einsum('acti,actj->iacj', volts, volts, preferred_element_type=jnp.fl...  11 us
    unnamed x13, local copies, waits for them, and re-layouts  8.36 us
    all_to_all x1, waiting for transfers between devices, body(): lax.all_to_all(grouped, 'chan', split_axis=4, concat_axis=2, tiled=True)  7.86 us
  transfers between devices with their start and end apart: 3, of which 3 were waited for; matrix products, arithmetic and copies ran while one was open for 1% of the time, Pallas kernels for 0%

commit v1 on v0

--- a/solution.py
+++ b/solution.py
@@ -116,7 +116,11 @@
         time_devs * chan_devs * row_count, 2, col_width
     )
     normal_rows = lax.psum_scatter(arranged, ("tm", "chan"), scatter_dimension=0, tiled=True)
-    rhs_all = lax.psum(jnp.transpose(rhs_part.reshape(2, inputs), (1, 0)), ("tm", "chan"))
+
+    def sources_all_advance(xx, net_axis, across):
+        return lax.psum(lax.psum(xx, net_axis), across)
+
+    rhs_all = sources_all_advance(jnp.transpose(rhs_part.reshape(2, inputs), (1, 0)), "chan", "tm")
     rhs_rows = lax.dynamic_slice_in_dim(rhs_all, lax.axis_index("tm") * row_count, row_count, 0)
     columns = lax.axis_index("chan") * col_width + jnp.arange(col_width, dtype=jnp.int32)
     params = jnp.arange(2, dtype=jnp.int32)[None, :] * inputs + row_inputs[:, None]

time: 299 us -> 280 us (0.936)
  blocking collectives: 37.9 us -> 21.6 us
  waiting for transfers between devices: 184 us -> 181 us
    psum x1 -> x2, blocking collectives: 37.9 us -> 21.6 us  [sources_all_advance(): return lax.psum(lax.psum(xx, net_axis), across)]
    reduce_scatter x1, waiting for transfers between devices: 133 us -> 130 us  [body(): lax.psum_scatter(arranged, ('tm', 'chan'), scatter_dimension=0, tiled=True)]
where the time goes in v1:
time: 280 us; the launch traced here: 279 us
  waiting for transfers between devices  181 us (65%)
  other arithmetic  24.6 us (9%)
  blocking collectives  21.6 us (8%)
  local copies, waits for them, and re-layouts  19.4 us (7%)
  between operations  15 us (5%)
  matrix products  13.6 us (5%)
  starting transfers between devices  4.65 us (2%)
    reduce_scatter x1, waiting for transfers between devices, body(): lax.psum_scatter(arranged, ('tm', 'chan'), scatter_dimension=0, tiled=True)  130 us
    unnamed x3, waiting for transfers between devices  42.6 us
    psum x2, blocking collectives, sources_all_advance(): return lax.psum(lax.psum(xx, net_axis), across)  21.6 us
    reduce_sum x1, other arithmetic, fringe_window(): fre = jnp.sum(vr * cosine + vi * sine, axis=(4, 5))  16.5 us
    dot_general x1, matrix products, full_gram(): jnp.einsum('acti,actj->iacj', volts, volts, preferred_element_type=jnp.fl...  11 us
    unnamed x13, local copies, waits for them, and re-layouts  8.36 us
    all_to_all x1, waiting for transfers between devices, body(): lax.all_to_all(grouped, 'chan', split_axis=4, concat_axis=2, tiled=True)  7.86 us
  transfers between devices with their start and end apart: 3, of which 3 were waited for; matrix products, arithmetic and copies ran while one was open for 1% of the time, Pallas kernels for 0%

profile of v1, /device:TPU:0, one launch (start us, length us, event | category | flops | bytes accessed | tf_op | source)
XLA Modules:
  0.0 279.4 jit_solution(9168451399878245506)
XLA Ops:
  7.2 11.0 %convolution_bitcast_fusion = f32[256,4,4,256]{0,3,2,1:T(8,128)S(1)} fusion(bf16[4,4,1536,256]{3,2,1,0:T(8,128)(2,1)} %param.5), kind=kOutput, calls=%fused_computation.11 | convolution fusion | flops 3221225472 | bytes 16777216 | tf_op jit(solution)/shard_map/acti,actj->iacj/dot_general | solution.py:76
  19.0 1.9 copy.56
  22.3 42.6 %reduce-scatter.7.cloned.1.call-done = f32[16,4096]{1,0:T(8,128)} async-done(((f32[128,4096]{1,0:T(8,128)}), f32[16,4096]{1,0:T(8,128)}) %reduce-scatter.7.cloned.1.call-update) | async-done | bytes 262160
  64.9 1.5 copy.57
  66.5 2.7 copy.41
  69.2 4.9 %gather_fusion = f32[128,16,4,4,2]{1,3,4,2,0:T(4,128)} fusion(f32[16,4,4,2,128]{0,2,4,3,1:T(4,128)} %copy.41, s32[1024]{0:T(1024)S(1)} %pad_clamp_fusion), kind=kCustom, calls=%fused_computation | custom fusion | bytes 524800 | tf_op jit(solution)/shard_map/jit(_take)/gather | solution.py:101
  74.1 2.1 fusion.47
  76.2 2.3 reshape.374
  78.5 4.6 %all-to-all-start = ((f32[4,1,16384]{2,1,0:T(1,128)}), f32[4,1,16384]{2,1,0:T(1,128)S(1)}, u32[]{:S(2)}, u32[]{:S(2)}) async-start(f32[4,1,16384]{2,1,0:T(1,128)} %reshape.374), calls=%async_computation | async-start | bytes 524288 | tf_op jit(solution)/shard_map/all_to_all | solution.py:102
  83.1 1.0 fusion.22
  84.2 7.9 %all-to-all-done = f32[4,1,16384]{2,1,0:T(1,128)S(1)} async-done(((f32[4,1,16384]{2,1,0:T(1,128)}), f32[4,1,16384]{2,1,0:T(1,128)S(1)}, u32[]{:S(2)}, u32[]{:S(2)}) %all-to-all-start) | async-done | bytes 262176 | tf_op jit(solution)/shard_map/all_to_all | solution.py:102
  92.5 1.4 reduce
  93.9 1.5 reshape.375
  95.4 1.0 copy.42
  97.4 16.5 %fusion.5 = (f32[16,32,2,4]{1,3,2,0:T(4,128)S(1)}, f32[16,32,2,4]{1,3,2,0:T(4,128)S(1)}) fusion(f32[16,32,4,16]{1,3,2,0:T(8,128)S(1)} %copy.44, f32[16,32,4,16]{1,3,2,0:T(8,128)S(1)} %copy-done, f32[16,32,2,4]{1,3,2,0:T(4,128)S(1)} %fusion.41, f32[16,32,4,16]{1,3,2,0:T(8,128)S(1)} %copy.43), kind=kLoop, calls=%fused_computation.8 | loop fusion | flops 2351104 | bytes 442368 | tf_op jit(solution)/shard_map/reduce_sum | solution.py:34
  114.8 9.8 %psum.14 = f32[128,2]{0,1:T(2,128)S(1)} all-reduce(f32[128,2]{0,1:T(2,128)S(1)} %maximum_bitcast_fusion), channel_id=1, replica_groups=mesh['tm'=8,'chan'=4] {'chan'}, use_global_device_ids=true, to_apply=%region_9.10 | all-reduce | flops 256 | bytes 2048 | tf_op jit(solution)/shard_map/psum | solution.py:121
  124.6 11.8 %psum.15 = f32[128,2]{0,1:T(2,128)S(1)} all-reduce(f32[128,2]{0,1:T(2,128)S(1)} %psum.14), channel_id=1, replica_groups=mesh['tm'=8,'chan'=4] {'tm'}, use_global_device_ids=true, to_apply=%region_10.11 | all-reduce | flops 256 | bytes 2048 | tf_op jit(solution)/shard_map/psum | solution.py:121
  136.4 0.7 fusion.9
  137.0 0.7 fusion.8
  137.7 0.7 fusion.10
  138.8 0.8 copy.48
  139.7 0.7 pad_maximum_fusion
  141.0 130.2 %reduce-scatter.5.cloned.1.call-done = f32[16,2,64]{2,0,1:T(8,128)} async-done(((f32[512,2,64]{2,0,1:T(8,128)}), f32[16,2,64]{2,0,1:T(8,128)}) %reduce-scatter.5.cloned.1.call-update) | async-done | bytes 8208 | tf_op jit(solution)/shard_map/reduce_scatter | solution.py:118
  271.2 0.8 convert_select_fusion
  (54 shorter events, 5.6 us)
Async XLA Ops:
  7.2 57.8 %reduce-scatter.7.cloned.1.call-start = ((), (), s32[]{:S(2)}) async-start(), calls=%async_computation.4 | async-start | bytes 2359296
  19.0 2.6 copy-start.3
  19.0 3.1 %copy-start.1 = (s32[16,32]{1,0:T(8,128)S(1)}, s32[16,32]{1,0:T(8,128)}, u32[]{:S(2)}) copy-start(s32[16,32]{1,0:T(8,128)} %param.7) | copy-start | bytes 6148
  19.0 3.2 %copy-start.2 = (s32[16,32]{1,0:T(8,128)S(1)}, s32[16,32]{1,0:T(8,128)}, u32[]{:S(2)}) copy-start(s32[16,32]{1,0:T(8,128)} %param.6) | copy-start | bytes 6148
  78.5 13.5 %all-to-all-start = ((f32[4,1,16384]{2,1,0:T(1,128)}), f32[4,1,16384]{2,1,0:T(1,128)S(1)}, u32[]{:S(2)}, u32[]{:S(2)}) async-start(f32[4,1,16384]{2,1,0:T(1,128)} %reshape.374), calls=%async_computation | async-start | bytes 524288 | tf_op jit(solution)/shard_map/all_to_all | solution.py:102
  83.1 188.1 %reduce-scatter.5.cloned.1.call-start = ((), (), s32[]{:S(2)}) async-start(), calls=%async_computation.3 | async-start | bytes 540672 | tf_op jit(solution)/shard_map/reduce_scatter | solution.py:118
  96.4 1.0 copy-start
Sparse Core Ops, SparseCore 0:
  21.0 43.8 reduce-scatter.6
  139.8 131.3 reduce-scatter.4
